TPU v7x, 32 devices: a whole 2x2x4 slice. The times are simulated.
32 devices in a mesh: space: 4 (over y, x), exc: 8 (over z, core).
Axes of the slice: x: 2, y: 2, z: 4, core: 2. Of those that a mesh axis runs over, the one named last changes fastest.
Arguments:
- coeff: float32 [64, 256, 4096], P('space', None, 'exc'), may hold values from -6 to 6
- factors: float32 [4, 64, 256, 512], P(None, 'space', 'exc'), may hold values from -0.25 to 0.25
Outputs:
- applied: float32 [64, 256, 4096], P('space', None, 'exc')
All inputs are finite; a program needn't handle non-finite values.
Results may differ from a plain program's by a relative error of at most 0.0003.
Values sent between devices are 32-bit elements; how exact they have to be, the bound alone decides.
A program may use at most 128 MiB of HBM per device.

v0:
```python
import jax
import jax.numpy as jnp
from jax import lax
from jax.sharding import PartitionSpec as P

BITS = 6
LEVELS = 4


def paired(state, bit):
    count = state.shape[0]
    stride = 1 << bit
    shaped = state.reshape(count // (2 * stride), 2, stride, state.shape[1], state.shape[2])
    return shaped[:, ::-1].reshape(state.shape)


def contract(rows, state, other):
    stacked = jnp.concatenate([state, other], axis=1)
    return jnp.einsum(
        "brk,bke->bre",
        rows,
        stacked,
        precision=lax.Precision.HIGHEST,
        preferred_element_type=jnp.float32,
    )


def level_product(rows_dev, state, other):
    return contract(lax.all_gather(rows_dev, "exc", axis=1, tiled=True), state, other)


def regroup(state, groups):
    shaped = state.reshape(groups, state.shape[0] // groups, state.shape[1], state.shape[2])
    return lax.all_to_all(shaped, "space", split_axis=0, concat_axis=0, tiled=True).reshape(
        state.shape
    )


def restore(state, groups):
    shaped = state.reshape(groups, state.shape[0] // groups, state.shape[1], state.shape[2])
    return lax.all_to_all(shaped, "space", split_axis=0, concat_axis=0, tiled=True).reshape(
        state.shape
    )


def body(coeff, factors):
    blocks_dev = coeff.shape[0]
    local_bits = blocks_dev.bit_length() - 1
    groups = lax.axis_size("space")
    group_bits = groups.bit_length() - 1
    first_bit = BITS - LEVELS
    cross_start = min(LEVELS, max(0, local_bits - first_bit))
    level_rows = [factors[level] for level in range(LEVELS)]
    moved = factors[cross_start:]
    shaped = moved.reshape(
        moved.shape[0], groups, blocks_dev // groups, moved.shape[2], moved.shape[3]
    )
    shaped = lax.all_to_all(shaped, "space", split_axis=1, concat_axis=1, tiled=True).reshape(
        moved.shape
    )
    level_rows = level_rows[:cross_start] + [shaped[index] for index in range(LEVELS - cross_start)]
    state = coeff
    for level in range(LEVELS):
        bit = first_bit + level
        if bit < local_bits:
            other = paired(state, bit)
        else:
            if level == cross_start:
                state = regroup(state, groups)
            other = paired(state, bit - group_bits)
        state = level_product(level_rows[level], state, other)
    state = restore(state, groups)
    return state


def solution(mesh):
    return jax.shard_map(
        body,
        mesh=mesh,
        in_specs=(P("space", None, "exc"), P(None, "space", "exc", None)),
        out_specs=P("space", None, "exc"),
        check_vma=False,
    )
```

profile of v0, /device:TPU:0, one launch (start us, length us, event | category | flops | bytes accessed | tf_op | source)
XLA Modules:
  0.0 523.2 jit_solution(10234973929096856032)
XLA Ops:
  6.5 0.0 slice-start
  6.5 0.0 all-gather.11.cloned.1.call-start
  6.5 3.3 fusion.22
  9.8 0.0 all-gather.11.cloned.1.call-update
  9.9 0.0 all-gather.13.cloned.1.call-start
  9.9 0.7 all-gather.13.cloned.1.call-update
  10.6 0.0 all-gather.7.cloned.1.call-start
  10.7 0.0 slice-done
  10.7 0.2 copy.16
  10.9 30.4 %all_to_all.15 = f32[2,4,4,32,512]{4,3,2,0,1:T(8,128)S(1)} all-to-all(f32[2,4,4,32,512]{4,3,2,0,1:T(8,128)S(1)} %copy.16), channel_id=1, replica_groups=mesh['space'=4,'exc'=8] {'space'}, dimensions={1} | all-to-all | bytes 4194304 | tf_op jit(solution)/shard_map/all_to_all | solution.py:58
  41.3 1.6 fusion.23
  42.8 0.0 all-gather.7.cloned.1.call-update
  42.8 0.0 all-gather.9.cloned.1.call-start
  42.9 0.5 all-gather.9.cloned.1.call-update
  43.4 8.3 %rev.12 = f32[2,2,4,256,512]{4,3,2,1,0:T(8,128)} reverse(f32[2,2,4,256,512]{4,3,2,1,0:T(8,128)} %bitcast.36), dimensions={1} | reverse | bytes 16777216 | tf_op jit(solution)/shard_map/rev | solution.py:14
  51.7 43.1 %all-gather.11.cloned.1.call-done = f32[1,16,256,512]{3,2,1,0:T(8,128)} async-done(((f32[1,16,32,512]{3,2,1,0:T(8,128)}), f32[1,16,256,512]{3,2,1,0:T(8,128)}) %all-gather.11.cloned.1.call-update) | async-done | bytes 8388624 | tf_op jit(solution)/shard_map/all_gather | solution.py:29
  94.8 22.3 %fusion = f32[16,512,256]{1,2,0:T(8,128)} fusion(f32[16,256,512]{2,1,0:T(8,128)} %bitcast.41, f32[16,256,512]{2,1,0:T(8,128)} %param.2, f32[1,16,256,512]{3,2,1,0:T(8,128)} %all-gather.11.cloned.1.call-done), kind=kOutput, calls=%fused_computation | convolution fusion | flops 12889096192 | bytes 33554432 | tf_op jit(solution)/shard_map/brk,bke->bre/dot_general | solution.py:19
  117.1 8.1 %rev.13 = f32[1,2,8,256,512]{4,3,2,1,0:T(8,128)} reverse(f32[1,2,8,256,512]{4,3,2,1,0:T(8,128)} %bitcast.34), dimensions={1} | reverse | bytes 16777216 | tf_op jit(solution)/shard_map/rev | solution.py:14
  125.2 51.7 %all-gather.13.cloned.1.call-done = f32[1,16,256,512]{3,2,1,0:T(8,128)} async-done(((f32[1,16,32,512]{3,2,1,0:T(8,128)}), f32[1,16,256,512]{3,2,1,0:T(8,128)}) %all-gather.13.cloned.1.call-update) | async-done | bytes 8388624 | tf_op jit(solution)/shard_map/all_gather | solution.py:29
  176.9 35.8 %fusion.4 = f32[16,512,256]{2,1,0:T(8,128)} fusion(f32[16,256,512]{2,1,0:T(8,128)} %bitcast.39, f32[16,256,512]{2,1,0:T(8,128)} %bitcast.35, f32[1,16,256,512]{3,2,1,0:T(8,128)} %all-gather.13.cloned.1.call-done), kind=kOutput, calls=%fused_computation.4 | convolution fusion | flops 12889096192 | bytes 33554432 | tf_op jit(solution)/shard_map/brk,bke->bre/dot_general | solution.py:19
  212.7 101.0 %all_to_all.16 = f32[4,4,256,512]{2,3,1,0:T(8,128)} all-to-all(f32[4,4,256,512]{2,3,1,0:T(8,128)} %bitcast.42), channel_id=1, replica_groups=mesh['space'=4,'exc'=8] {'space'}, dimensions={0} | all-to-all | bytes 16777216 | tf_op jit(solution)/shard_map/all_to_all | solution.py:34
  313.7 9.9 %copy.15 = f32[2,2,4,256,512]{4,3,2,1,0:T(8,128)} copy(f32[2,2,4,256,512]{3,4,2,1,0:T(8,128)} %bitcast.31) | data formatting | bytes 16777216 | tf_op jit(solution)/shard_map/reshape;reshape | solution.py:13
  323.5 8.0 %rev.14 = f32[2,2,4,256,512]{4,3,2,1,0:T(8,128)} reverse(f32[2,2,4,256,512]{4,3,2,1,0:T(8,128)} %copy.15), dimensions={1} | reverse | bytes 16777216 | tf_op jit(solution)/shard_map/rev | solution.py:14
  331.6 9.9 %copy.14 = f32[4,4,256,512]{3,2,1,0:T(8,128)} copy(f32[4,4,256,512]{2,3,1,0:T(8,128)} %all_to_all.16) | data formatting | bytes 16777216 | tf_op jit(solution)/shard_map/all_to_all | solution.py:34
  341.5 0.0 all-gather.7.cloned.1.call-done
  341.5 21.6 %fusion.8 = f32[16,512,256]{1,2,0:T(8,128)} fusion(f32[16,256,512]{2,1,0:T(8,128)} %all-gather.7.cloned.1.call-done, f32[16,256,512]{2,1,0:T(8,128)} %bitcast.37, f32[16,256,512]{2,1,0:T(8,128)} %bitcast.38), kind=kOutput, calls=%fused_computation.8 | convolution fusion | flops 12889096192 | bytes 33554432 | tf_op jit(solution)/shard_map/brk,bke->bre/dot_general | solution.py:19
  363.1 8.1 %rev.15 = f32[1,2,8,256,512]{4,3,2,1,0:T(8,128)} reverse(f32[1,2,8,256,512]{4,3,2,1,0:T(8,128)} %bitcast.32), dimensions={1} | reverse | bytes 16777216 | tf_op jit(solution)/shard_map/rev | solution.py:14
  371.2 0.0 all-gather.9.cloned.1.call-done
  371.2 35.4 %fusion.12 = f32[16,512,256]{2,1,0:T(8,128)} fusion(f32[16,256,512]{2,1,0:T(8,128)} %all-gather.9.cloned.1.call-done, f32[16,256,512]{2,1,0:T(8,128)} %bitcast.40, f32[16,256,512]{2,1,0:T(8,128)} %bitcast.33), kind=kOutput, calls=%fused_computation.12 | convolution fusion | flops 12889096192 | bytes 33554432 | tf_op jit(solution)/shard_map/brk,bke->bre/dot_general | solution.py:19
  406.6 99.8 %all_to_all.17 = f32[4,4,256,512]{2,3,1,0:T(8,128)} all-to-all(f32[4,4,256,512]{2,3,1,0:T(8,128)} %bitcast.43), channel_id=1, replica_groups=mesh['space'=4,'exc'=8] {'space'}, dimensions={0} | all-to-all | bytes 16777216 | tf_op jit(solution)/shard_map/all_to_all | solution.py:41
  506.4 9.9 %copy.18 = f32[4,4,256,512]{3,2,1,0:T(8,128)} copy(f32[4,4,256,512]{2,3,1,0:T(8,128)} %all_to_all.17) | data formatting | bytes 16777216 | tf_op jit(solution)/shard_map/all_to_all | solution.py:41
Async XLA Ops:
  6.5 4.1 slice-start
  6.5 88.2 %all-gather.11.cloned.1.call-start = ((), (), s32[]{:S(2)}) async-start(), calls=%async_computation.5 | async-start | bytes 9437184 | tf_op jit(solution)/shard_map/all_gather | solution.py:29
  9.9 167.1 %all-gather.13.cloned.1.call-start = ((), (), s32[]{:S(2)}) async-start(), calls=%async_computation.6 | async-start | bytes 9437184 | tf_op jit(solution)/shard_map/all_gather | solution.py:29
  10.6 330.9 %all-gather.7.cloned.1.call-start = ((), (), s32[]{:S(2)}) async-start(), calls=%async_computation.3 | async-start | bytes 9437184 | tf_op jit(solution)/shard_map/all_gather | solution.py:29
  42.8 328.4 %all-gather.9.cloned.1.call-start = ((), (), s32[]{:S(2)}) async-start(), calls=%async_computation.4 | async-start | bytes 9437184 | tf_op jit(solution)/shard_map/all_gather | solution.py:29
Sparse Core Ops, SparseCore 0:
  10.0 84.7 all-gather.10
  96.4 80.5 all-gather.12
  178.5 80.5 all-gather.6
  260.6 80.5 all-gather.8
where the time goes:
time: 530 us; the launch traced here: 523 us
  blocking collectives  231 us (44%)
  matrix products  115 us (22%)
  waiting for transfers between devices  96.1 us (18%)
  local copies, waits for them, and re-layouts  67.3 us (13%)
  between operations  13.5 us (3%)
    dot_general x4, matrix products, contract(): jnp.einsum('brk,bke->bre', rows, stacked, precision=lax.Precision.HIGHEST...  115 us
    all_to_all x1, blocking collectives, regroup(): lax.all_to_all(shaped, 'space', split_axis=0, concat_axis=0, tiled=True)  101 us
    all_to_all x1, blocking collectives, restore(): lax.all_to_all(shaped, 'space', split_axis=0, concat_axis=0, tiled=True)  99.8 us
    all_gather x4, waiting for transfers between devices, level_product(): lax.all_gather(rows_dev, 'exc', axis=1, tiled=True)  94.8 us
    rev x4, local copies, waits for them, and re-layouts, paired(): return shaped[:, ::-1].reshape(state.shape)  32.5 us
    all_to_all x1, blocking collectives, body(): lax.all_to_all(shaped, 'space', split_axis=1, concat_axis=1, tiled=True)  30.4 us
  transfers between devices with their start and end apart: 4, of which 2 were waited for; matrix products, arithmetic and copies ran while one was open for 26% of the time, Pallas kernels for 0%

commit v1 on v0

--- a/solution.py
+++ b/solution.py
@@ -55,9 +55,10 @@
     shaped = moved.reshape(
         moved.shape[0], groups, blocks_dev // groups, moved.shape[2], moved.shape[3]
     )
-    shaped = lax.all_to_all(shaped, "space", split_axis=1, concat_axis=1, tiled=True).reshape(
-        moved.shape
-    )
+    shaped = jnp.concatenate(
+        lax.all_to_all(jnp.stack(jnp.split(shaped, lax.axis_size("space"), axis=1)), "space", 0, 0),
+        axis=1,
+    ).reshape(moved.shape)
     level_rows = level_rows[:cross_start] + [shaped[index] for index in range(LEVELS - cross_start)]
     state = coeff
     for level in range(LEVELS):

time: 530 us -> 499 us (0.942); the launches traced: 523 us -> 498 us
  matrix products: 115 us -> 100 us
  local copies, waits for them, and re-layouts: 67.3 us -> 60.8 us
    dot_general x4, matrix products: 115 us -> 100 us  [contract(): jnp.einsum('brk,bke->bre', rows, stacked, precision=lax.Precision.HIGHEST...]
    all_to_all x1 -> x0, local copies, waits for them, and re-layouts: 9.87 us -> none  [restore(): lax.all_to_all(shaped, 'space', split_axis=0, concat_axis=0, tiled=True)]
  transfers between devices with their start and end apart: 4 -> 4, of which waited for: 2 -> 2; matrix products, arithmetic and copies ran while one was open for 26% -> 27% of each run, Pallas kernels for 0% -> 0%
where the time goes in v1:
time: 499 us; the launch traced here: 498 us
  blocking collectives  228 us (46%)
  matrix products  100 us (20%)
  waiting for transfers between devices  95.8 us (19%)
  local copies, waits for them, and re-layouts  60.8 us (12%)
  between operations  13.2 us (3%)
    all_to_all x1, blocking collectives, regroup(): lax.all_to_all(shaped, 'space', split_axis=0, concat_axis=0, tiled=True)  101 us
    dot_general x4, matrix products, contract(): jnp.einsum('brk,bke->bre', rows, stacked, precision=lax.Precision.HIGHEST...  100 us
    all_to_all x1, blocking collectives, restore(): lax.all_to_all(shaped, 'space', split_axis=0, concat_axis=0, tiled=True)  96.3 us
    all_gather x4, waiting for transfers between devices, level_product(): lax.all_gather(rows_dev, 'exc', axis=1, tiled=True)  94.6 us
    rev x4, local copies, waits for them, and re-layouts, paired(): return shaped[:, ::-1].reshape(state.shape)  32.5 us
    all_to_all x1, blocking collectives, body(): lax.all_to_all(jnp.stack(jnp.split(shaped, lax.axis_size('space'), axis=1...  30.4 us
  transfers between devices with their start and end apart: 4, of which 2 were waited for; matrix products, arithmetic and copies ran while one was open for 27% of the time, Pallas kernels for 0%

profile of v1, /device:TPU:0, one launch (start us, length us, event | category | flops | bytes accessed | tf_op | source)
XLA Modules:
  0.0 498.1 jit_solution(5611487796487392587)
XLA Ops:
  6.5 0.0 slice-start
  6.5 0.0 all-gather.11.cloned.1.call-start
  6.5 3.3 fusion.22
  9.8 0.0 all-gather.11.cloned.1.call-update
  9.9 0.0 all-gather.13.cloned.1.call-start
  9.9 0.7 all-gather.13.cloned.1.call-update
  10.6 0.0 all-gather.9.cloned.1.call-start
  10.7 0.0 slice-done
  10.7 0.2 slice_bitcast_fusion.3
  10.9 0.3 maximum_bitcast_fusion
  11.2 30.4 %all_to_all.15 = f32[4,2,1,4,32,512]{5,4,3,2,1,0:T(8,128)S(1)} all-to-all(f32[4,2,1,4,32,512]{5,4,3,2,1,0:T(8,128)S(1)} %maximum_bitcast_fusion), channel_id=1, replica_groups=mesh['space'=4,'exc'=8] {'space'}, dimensions={0} | all-to-all | bytes 4194304 | tf_op jit(solution)/shard_map/all_to_all | solution.py:59
  41.5 1.5 fusion.23
  43.1 0.0 all-gather.9.cloned.1.call-update
  43.1 0.0 all-gather.7.cloned.1.call-start
  43.2 0.5 all-gather.7.cloned.1.call-update
  43.7 8.2 %rev.12 = f32[2,2,4,256,512]{4,3,2,1,0:T(8,128)} reverse(f32[2,2,4,256,512]{4,3,2,1,0:T(8,128)} %bitcast.49), dimensions={1} | reverse | bytes 16777216 | tf_op jit(solution)/shard_map/rev | solution.py:14
  51.9 42.8 %all-gather.11.cloned.1.call-done = f32[1,16,256,512]{3,2,1,0:T(8,128)} async-done(((f32[1,16,32,512]{3,2,1,0:T(8,128)}), f32[1,16,256,512]{3,2,1,0:T(8,128)}) %all-gather.11.cloned.1.call-update) | async-done | bytes 8388624 | tf_op jit(solution)/shard_map/all_gather | solution.py:29
  94.8 22.3 %fusion = f32[16,512,256]{1,2,0:T(8,128)} fusion(f32[16,256,512]{2,1,0:T(8,128)} %bitcast.54, f32[16,256,512]{2,1,0:T(8,128)} %param.2, f32[1,16,256,512]{3,2,1,0:T(8,128)} %all-gather.11.cloned.1.call-done), kind=kOutput, calls=%fused_computation | convolution fusion | flops 12889096192 | bytes 33554432 | tf_op jit(solution)/shard_map/brk,bke->bre/dot_general | solution.py:19
  117.1 8.1 %rev.13 = f32[1,2,8,256,512]{4,3,2,1,0:T(8,128)} reverse(f32[1,2,8,256,512]{4,3,2,1,0:T(8,128)} %bitcast.46), dimensions={1} | reverse | bytes 16777216 | tf_op jit(solution)/shard_map/rev | solution.py:14
  125.2 51.7 %all-gather.13.cloned.1.call-done = f32[1,16,256,512]{3,2,1,0:T(8,128)} async-done(((f32[1,16,32,512]{3,2,1,0:T(8,128)}), f32[1,16,256,512]{3,2,1,0:T(8,128)}) %all-gather.13.cloned.1.call-update) | async-done | bytes 8388624 | tf_op jit(solution)/shard_map/all_gather | solution.py:29
  176.9 35.5 %fusion.4 = f32[16,512,256]{2,1,0:T(8,128)} fusion(f32[16,256,512]{2,1,0:T(8,128)} %bitcast.52, f32[16,256,512]{2,1,0:T(8,128)} %bitcast.47, f32[1,16,256,512]{3,2,1,0:T(8,128)} %all-gather.13.cloned.1.call-done), kind=kOutput, calls=%fused_computation.4 | convolution fusion | flops 12889096192 | bytes 33554432 | tf_op jit(solution)/shard_map/brk,bke->bre/dot_general | solution.py:19
  212.4 100.9 %all_to_all.16 = f32[4,4,256,512]{2,3,1,0:T(8,128)} all-to-all(f32[4,4,256,512]{2,3,1,0:T(8,128)} %bitcast.55), channel_id=1, replica_groups=mesh['space'=4,'exc'=8] {'space'}, dimensions={0} | all-to-all | bytes 16777216 | tf_op jit(solution)/shard_map/all_to_all | solution.py:34
  313.3 9.9 %copy.22 = f32[2,2,4,256,512]{4,3,2,1,0:T(8,128)} copy(f32[2,2,4,256,512]{3,4,2,1,0:T(8,128)} %bitcast.44) | data formatting | bytes 16777216 | tf_op jit(solution)/shard_map/reshape;reshape | solution.py:13
  323.3 8.0 %rev.14 = f32[2,2,4,256,512]{4,3,2,1,0:T(8,128)} reverse(f32[2,2,4,256,512]{4,3,2,1,0:T(8,128)} %copy.22), dimensions={1} | reverse | bytes 16777216 | tf_op jit(solution)/shard_map/rev | solution.py:14
  331.3 9.9 %copy.21 = f32[4,4,256,512]{3,2,1,0:T(8,128)} copy(f32[4,4,256,512]{2,3,1,0:T(8,128)} %all_to_all.16) | data formatting | bytes 16777216 | tf_op jit(solution)/shard_map/all_to_all | solution.py:34
  341.2 0.0 all-gather.9.cloned.1.call-done
  341.2 21.2 %fusion.8 = f32[16,256,512]{2,1,0:T(8,128)} fusion(f32[16,256,512]{2,1,0:T(8,128)} %all-gather.9.cloned.1.call-done, f32[16,256,512]{2,1,0:T(8,128)} %bitcast.50, f32[16,256,512]{2,1,0:T(8,128)} %bitcast.51), kind=kOutput, calls=%fused_computation.8 | convolution fusion | flops 12889096192 | bytes 33554432 | tf_op jit(solution)/shard_map/brk,bke->bre/dot_general | solution.py:19
  362.4 8.1 %rev.15 = f32[1,2,8,256,512]{4,3,2,1,0:T(8,128)} reverse(f32[1,2,8,256,512]{4,3,2,1,0:T(8,128)} %bitcast.45), dimensions={1} | reverse | bytes 16777216 | tf_op jit(solution)/shard_map/rev | solution.py:14
  370.6 0.0 all-gather.7.cloned.1.call-done
  370.6 21.2 %fusion.12 = f32[16,256,512]{2,1,0:T(8,128)} fusion(f32[16,256,512]{2,1,0:T(8,128)} %all-gather.7.cloned.1.call-done, f32[16,256,512]{2,1,0:T(8,128)} %bitcast.53, f32[16,256,512]{2,1,0:T(8,128)} %fusion.8), kind=kOutput, calls=%fused_computation.12 | convolution fusion | flops 12889096192 | bytes 33554432 | tf_op jit(solution)/shard_map/brk,bke->bre/dot_general | solution.py:19
  391.8 96.3 %all_to_all.17 = f32[4,4,256,512]{3,2,1,0:T(8,128)S(1)} all-to-all(f32[4,4,256,512]{3,2,1,0:T(8,128)} %bitcast.56), channel_id=1, replica_groups=mesh['space'=4,'exc'=8] {'space'}, dimensions={0} | all-to-all | bytes 16777216 | tf_op jit(solution)/shard_map/all_to_all | solution.py:41
  488.1 3.4 copy.28
Async XLA Ops:
  6.5 4.1 slice-start
  6.5 88.2 %all-gather.11.cloned.1.call-start = ((), (), s32[]{:S(2)}) async-start(), calls=%async_computation.5 | async-start | bytes 9437184 | tf_op jit(solution)/shard_map/all_gather | solution.py:29
  9.9 167.1 %all-gather.13.cloned.1.call-start = ((), (), s32[]{:S(2)}) async-start(), calls=%async_computation.6 | async-start | bytes 9437184 | tf_op jit(solution)/shard_map/all_gather | solution.py:29
  10.6 330.6 %all-gather.9.cloned.1.call-start = ((), (), s32[]{:S(2)}) async-start(), calls=%async_computation.4 | async-start | bytes 9437184 | tf_op jit(solution)/shard_map/all_gather | solution.py:29
  43.1 327.4 %all-gather.7.cloned.1.call-start = ((), (), s32[]{:S(2)}) async-start(), calls=%async_computation.3 | async-start | bytes 9437184 | tf_op jit(solution)/shard_map/all_gather | solution.py:29
Sparse Core Ops, SparseCore 0:
  10.0 84.7 all-gather.10
  96.4 80.5 all-gather.12
  178.5 80.5 all-gather.8
  260.5 80.5 all-gather.6
